TPU v7x, 256 devices: a whole 4x4x8 slice. The times are simulated.
256 devices in a mesh: px: 32 (over z, x), py: 8 (over y, core).
Axes of the slice: x: 4, y: 4, z: 8, core: 2. Of those that a mesh axis runs over, the one named last changes fastest.
Arguments:
- counts: int32 [32], replicated, may hold values from 1 to 6, 64 in all
- coefficient: float32 [192, 8, 4096], P('px', 'py'), may hold values from 0.2 to 5
- signs: int32 [192, 8, 4096], P('px', 'py'), may hold values from 0 to 1
- basis_old: float32 [192, 8, 16, 4096], P('px', 'py'), may hold values from -8 to 8
- basis_last: float32 [192, 8, 16, 4096], P('px', 'py'), may hold values from -8 to 8
- residual_factor: float32 [16, 16], replicated, may hold values from -12 to 12
- previous_coef: float32 [32, 16], replicated, may hold values from -12 to 12
- sample_rows: int32 [2048], replicated, may hold values from 0 to 2097151, as said below
Outputs:
- new_block: float32 [192, 8, 16, 4096], P('px', 'py')
- sketch: float32 [48, 2048], P(None, ('px', 'py'))
- solution: float32 [32, 16], replicated
Inputs may be any that keep to these rules, and one draw needn't show every extreme that they name: Index i of px owns counts[i] consecutive patch columns, in px order; the largest count is exactly 6. `sample_rows`: distinct cell numbers, among them 0 and 2097151.
All inputs are finite; a program needn't handle non-finite values.
Results may differ from a plain program's by a relative error of at most 0.0003.
Values sent between devices are 32-bit elements; how exact they have to be, the bound alone decides.
No kernel may reach another device: no remote copies, remote signals or barrier semaphores. Data moves between devices by JAX's collectives and lax.ppermute only.
A program may use at most 256 MiB of HBM per device.

v0:
```python
import math
import jax
import jax.numpy as jnp
from jax import lax
from jax.sharding import PartitionSpec as P

PS = 16
K = 2048
MEANX = 2
CAP = 6
CELLS = 4096
highest = lax.Precision.HIGHEST


def extended(block, sides, width):
    for axis, dim in sides:
        count = lax.axis_size(axis)
        forward = [(i, i + 1) for i in range(count - 1)]
        backward = [(target, source) for source, target in forward]
        low = lax.ppermute(
            lax.slice_in_dim(block, block.shape[dim] - width, None, axis=dim), axis, forward
        )
        high = lax.ppermute(lax.slice_in_dim(block, 0, width, axis=dim), axis, backward)
        block = jnp.concatenate([low, block, high], axis=dim)
    return block


def parity_of(values):
    folded = values
    for amount in (16, 8, 4, 2, 1):
        folded = jnp.bitwise_xor(folded, jnp.right_shift(folded, amount))
    return jnp.bitwise_and(folded, 1)


def sign_table(length):
    indices = jnp.arange(length, dtype=jnp.int32)
    parity = parity_of(jnp.bitwise_and(indices[:, None], indices[None, :]))
    return (1 - 2 * parity).astype(jnp.float32)


def transform_cells(values):
    inner_len = min(CELLS, 128)
    outer_len = CELLS // inner_len
    shaped = values.reshape(values.shape[:-1] + (outer_len, inner_len))
    shaped = jnp.einsum("sjab,bd->sjad", shaped, sign_table(inner_len), precision=highest)
    shaped = jnp.einsum("ca,sjad->sjcd", sign_table(outer_len), shaped, precision=highest)
    return shaped.reshape(values.shape)


def shift_pair(cube_vals, low_plane, high_plane, axis_pos):
    below = jnp.concatenate(
        [
            jnp.expand_dims(low_plane, axis_pos),
            lax.slice_in_dim(cube_vals, 0, PS - 1, axis=axis_pos),
        ],
        axis=axis_pos,
    )
    above = jnp.concatenate(
        [lax.slice_in_dim(cube_vals, 1, PS, axis=axis_pos), jnp.expand_dims(high_plane, axis_pos)],
        axis=axis_pos,
    )
    return (below, above)


def apply_operator(last_local, kappa_local, held_count, slot_ids):
    channels = last_local.shape[1] + 1
    plane_size = PS * PS
    joined = jnp.concatenate([last_local, kappa_local[:, None]], axis=1)
    cube_vals = joined.reshape(CAP, channels, PS, PS, PS)
    first_face = cube_vals[0, :, 0].reshape(channels, plane_size)
    last_slot = lax.dynamic_index_in_dim(cube_vals, held_count - 1, 0, keepdims=False)
    last_face = last_slot[:, PS - 1].reshape(channels, plane_size)
    x_ghost = extended(jnp.stack([first_face, last_face]), (("px", 0),), 1)
    y_planes = jnp.stack([cube_vals[:, :, :, 0], cube_vals[:, :, :, PS - 1]]).reshape(
        2, CAP, channels, plane_size
    )
    y_ghost = extended(y_planes, (("py", 0),), 1)
    ghost_low = x_ghost[0].reshape(channels, PS, PS)
    ghost_high = x_ghost[3].reshape(channels, PS, PS)
    x_low = jnp.concatenate([ghost_low[None], cube_vals[:-1, :, PS - 1]], axis=0)
    next_faces = jnp.concatenate([cube_vals[1:, :, 0], jnp.zeros_like(cube_vals[:1, :, 0])], axis=0)
    x_high = jnp.where(
        (slot_ids == held_count - 1)[:, None, None, None], ghost_high[None], next_faces
    )
    y_low = y_ghost[0].reshape(CAP, channels, PS, PS)
    y_high = y_ghost[3].reshape(CAP, channels, PS, PS)
    z_zero = jnp.zeros((CAP, channels, PS, PS), jnp.float32)
    centre_vals = cube_vals[:, :-1]
    centre_kappa = cube_vals[:, -1:]
    diag_sum = jnp.zeros_like(centre_kappa)
    weighted = jnp.zeros_like(centre_vals)
    for low_plane, high_plane, axis_pos in (
        (x_low, x_high, 2),
        (y_low, y_high, 3),
        (z_zero, z_zero, 4),
    ):
        kappa_pair = shift_pair(centre_kappa, low_plane[:, -1:], high_plane[:, -1:], axis_pos)
        value_pair = shift_pair(centre_vals, low_plane[:, :-1], high_plane[:, :-1], axis_pos)
        for near_kappa, near_vals in zip(kappa_pair, value_pair):
            weight = 0.5 * (centre_kappa + near_kappa)
            diag_sum = diag_sum + weight
            weighted = weighted + weight * near_vals
    summed = diag_sum * centre_vals - weighted
    return summed.reshape(CAP, channels - 1, CELLS)


def normal_parts(sketch_cols, proj_coef, previous_coef, residual_factor):
    pair_count = proj_coef.shape[0]
    width_rhs = proj_coef.shape[1]
    pair_rows = sketch_cols[:pair_count]
    first_image = jnp.einsum("ab,ak->bk", previous_coef, pair_rows, precision=highest)
    second_image = (
        jnp.einsum("ab,ak->bk", proj_coef, pair_rows, precision=highest) + sketch_cols[pair_count:]
    )
    images = jnp.concatenate([first_image, second_image], axis=0)
    target = jnp.einsum("ab,ak->bk", residual_factor, sketch_cols[:width_rhs], precision=highest)
    return (
        jnp.dot(images, images.T, precision=highest),
        jnp.dot(images, target.T, precision=highest),
    )


def solve_normal(normal_gram, normal_cross):
    factor_low = jnp.linalg.cholesky(normal_gram)
    middle = lax.linalg.triangular_solve(factor_low, normal_cross, left_side=True, lower=True)
    return lax.linalg.triangular_solve(
        factor_low, middle, left_side=True, lower=True, transpose_a=True
    )


def body(
    counts, coefficient, signs, basis_old, basis_last, residual_factor, previous_coef, sample_rows
):
    px_index = lax.axis_index("px")
    py_index = lax.axis_index("py")
    py_count = lax.axis_size("py")
    device_count = lax.axis_size("px") * py_count
    total_cells = MEANX * device_count * CELLS
    offsets = jnp.cumsum(counts) - counts
    held_count = counts[px_index]
    slot_ids = jnp.arange(CAP, dtype=jnp.int32)
    live_weight = (slot_ids < held_count).astype(jnp.float32)
    old_local = basis_old[:, 0] * live_weight[:, None, None]
    last_local = basis_last[:, 0] * live_weight[:, None, None]
    image = (
        apply_operator(last_local, coefficient[:, 0], held_count, slot_ids)
        * live_weight[:, None, None]
    )
    pair = jnp.concatenate([old_local, last_local], axis=1)
    local_gram = jnp.einsum("sac,sbc->ab", pair, image, precision=highest)
    patch_ids = (offsets[px_index] + slot_ids) * py_count + py_index
    sign_flips = (1 - 2 * signs[:, 0]).astype(jnp.float32)
    share_width = K // device_count
    share_start = (px_index * py_count + py_index) * share_width
    proj_coef = lax.psum(local_gram, ("px", "py")) / total_cells
    new_local = image - jnp.einsum("sac,ab->sbc", pair, proj_coef, precision=highest)
    spread = transform_cells(jnp.concatenate([pair, new_local], axis=1) * sign_flips[:, None, :])
    picked = jnp.take(spread, sample_rows % CELLS, axis=2)
    parity = parity_of(jnp.bitwise_and(patch_ids[:, None], (sample_rows // CELLS)[None, :]))
    weights = (1 - 2 * parity).astype(jnp.float32) * live_weight[:, None]
    partial_value = jnp.einsum("sk,sjk->jk", weights, picked, precision=highest) * (
        1.0 / math.sqrt(total_cells)
    )
    sketch_whole = lax.psum(partial_value, ("px", "py"))
    sketch_mine = lax.dynamic_slice_in_dim(sketch_whole, share_start, share_width, 1)
    normal_gram, normal_cross = normal_parts(
        sketch_whole, proj_coef, previous_coef, residual_factor
    )
    solution = solve_normal(normal_gram, normal_cross)
    return (new_local[:, None], sketch_mine, solution)


def solution(mesh):
    in_specs = (
        P(),
        P("px", "py", None),
        P("px", "py", None),
        P("px", "py", None, None),
        P("px", "py", None, None),
        P(),
        P(),
        P(),
    )
    out_specs = (P("px", "py", None, None), P(None, ("px", "py")), P())
    return jax.shard_map(body, mesh=mesh, in_specs=in_specs, out_specs=out_specs, check_vma=False)
```

profile of v0, /device:TPU:1, one launch (start us, length us, event | category | flops | bytes accessed | tf_op | source)
XLA Modules:
  0.0 603.8 jit_solution(3196232569332509484)
XLA Ops:
  14.0 8.6 %reshape.92 = f32[6,17,16,16,16]{4,3,2,0,1:T(8,128)} reshape(f32[6,17,4096]{2,0,1:T(8,128)} %copy.21) | data formatting | bytes 3342336 | tf_op jit(solution)/shard_map/reshape | solution.py:69
  26.3 3.2 constant_dynamic-slice_fusion.1
  29.5 3.9 copy.22
  34.3 5.2 collective-permute-start
  39.5 10.8 %slice_reduce_fusion = (f32[6,17,16,16]{3,2,0,1:T(8,128)}, f32[6,17,16,16]{3,2,0,1:T(8,128)}) fusion(f32[6,17,16,16,16]{4,3,2,0,1:T(8,128)} %reshape.92), kind=kLoop, calls=%fused_computation.34 | loop fusion | bytes 417792 | tf_op jit(solution)/shard_map/slice | solution.py:74
  52.5 4.6 collective-permute-start.2
  59.3 3.0 collective-permute-start.3
  62.4 17.5 %fusion.102 = (f32[6,16,15,16,16]{4,3,2,0,1:T(8,128)}, f32[6,16,15,16,16]{4,3,2,0,1:T(8,128)}) fusion(f32[6,17,16,16,16]{4,3,2,0,1:T(8,128)} %reshape.92), kind=kLoop, calls=%fused_computation.173 | loop fusion | bytes 5898240 | tf_op jit(solution)/shard_map/slice | solution.py:59
  81.1 9.2 %fusion.101 = (f32[6,16,16,15,16]{4,3,2,0,1:T(8,128)}, f32[6,16,16,15,16]{4,3,2,0,1:T(8,128)}) fusion(f32[6,17,16,16,16]{4,3,2,0,1:T(8,128)S(1)} %bitcast.139), kind=kLoop, calls=%fused_computation.172 | loop fusion | bytes 5898240 | tf_op jit(solution)/shard_map/slice | solution.py:59
  90.3 9.8 %fusion.100 = (f32[6,16,16,16,15]{4,3,2,0,1:T(8,128)}, f32[6,16,16,16,15]{4,3,2,0,1:T(8,128)}) fusion(f32[6,17,16,16,16]{4,3,2,0,1:T(8,128)S(1)} %bitcast.139), kind=kLoop, calls=%fused_computation.171 | loop fusion | bytes 5898240 | tf_op jit(solution)/shard_map/slice | solution.py:54
  109.1 4.0 bitcast_multiply_fusion.1
  118.9 3.5 fusion.30
  134.3 5.0 add_bitcast_fusion
  139.3 37.8 %fusion = f32[6,16,16,16,16]{4,3,2,0,1:T(8,128)} fusion(f32[6,17,16,16,16]{4,3,2,0,1:T(8,128)} %reshape.92, f32[6,16,15,16,16]{4,3,2,0,1:T(8,128)} %get-tuple-element.29, f32[6,16,1,16,16]{4,3,2,0,1:T(8,128)} %get-tuple-element.41, f32[6,16,1,16,16]{4,3,2,0,1:T(8,128)} %get-tuple-element.40, f32[6,16,15,16,16]{4,3,2,0,1:T(8,128)} %get-tuple-element.28, ...), kind=kLoop, calls=%fused_computation.2 | loop fusion | flops 6684672 | bytes 13074432 | tf_op jit(solution)/shard_map/sub | solution.py:103
  177.1 10.5 %reshape.114 = f32[6,16,4096]{2,0,1:T(8,128)} reshape(f32[6,16,16,16,16]{4,3,2,0,1:T(8,128)} %fusion) | data formatting | bytes 3145728 | tf_op jit(solution)/shard_map/reshape | solution.py:104
  187.6 4.7 fusion.14
  192.3 80.0 %psum.14 = f32[32,16]{0,1:T(8,128)S(1)} all-reduce(f32[32,16]{0,1:T(8,128)S(1)} %fusion.14), channel_id=1, replica_groups=mesh['px'=32,'py'=8] {'px','py'}, use_global_device_ids=true, to_apply=%region_0.0 | all-reduce | flops 512 | bytes 4096 | tf_op jit(solution)/shard_map/psum | solution.py:155
  272.4 4.1 fusion.6
  277.6 4.0 fusion.7
  281.6 5.7 convolution_bitcast_fusion.1
  287.3 9.7 %copy.50 = f32[6,48,32,128]{1,0,3,2:T(8,128)} copy(f32[6,48,32,128]{3,2,1,0:T(8,128)} %convolution_bitcast_fusion.1) | data formatting | bytes 9437184 | tf_op jit(solution)/shard_map/reshape | solution.py:47
  297.0 21.6 %gather_fusion = f32[2048,6,48]{2,1,0:T(8,128)} fusion(f32[6,48,4096]{1,0,2:T(8,128)} %bitcast.140, s32[2048]{0:T(1024)S(1)} %copy-done.10), kind=kCustom, calls=%fused_computation | custom fusion | bytes 4726784 | tf_op jit(solution)/shard_map/jit(_take)/gather | solution.py:158
  318.6 13.2 %multiply_reduce_fusion = f32[2048,48]{1,0:T(8,128)S(1)} fusion(f32[2048,6,48]{2,1,0:T(8,128)} %gather_fusion, f32[2048,6]{1,0:T(8,128)S(1)} %copy-done.7, pred[2048]{0:T(1024)(128)(4,1)S(1)} %copy-done.15), kind=kLoop, calls=%fused_computation.12 | loop fusion | flops 1671168 | bytes 2803712
  333.0 248.0 %all-reduce.7.cloned.1.call-done = f32[48,2048]{1,0:T(8,128)} async-done(((f32[48,2048]{1,0:T(8,128)}), f32[48,2048]{1,0:T(8,128)}) %all-reduce.7.cloned.1.call-update) | async-done | bytes 393232 | tf_op jit(solution)/shard_map/psum | solution.py:164
  (115 shorter events, 60.2 us)
Async XLA Ops:
  7.2 576.6 %copy-start = (f32[32,16]{0,1:T(8,128)S(1)}, f32[32,16]{0,1:T(8,128)}, u32[]{:S(2)}) copy-start(f32[32,16]{0,1:T(8,128)} %param.14) | copy-start | bytes 6148
  7.2 4.3 copy-start.9
  7.2 573.8 %all-reduce.7.cloned.1.call-start = ((), (), s32[]{:S(2)}) async-start(), calls=%async_computation | async-start | bytes 786432 | tf_op jit(solution)/shard_map/psum | solution.py:164
  9.1 104.6 %copy-start.12 = (f32[6]{0:T(128)}, f32[6]{0:T(128)S(1)}, u32[]{:S(2)}) copy-start(f32[6]{0:T(128)S(1)} %compare_convert_fusion) | copy-start | bytes 76
  23.7 92.0 %collective-permute-start.1 = (f32[1,17,256]{2,0,1:T(1,128)S(1)}, f32[1,17,256]{2,0,1:T(1,128)S(1)}, u32[]{:S(2)}, u32[]{:S(2)}) collective-permute-start(f32[1,17,256]{2,0,1:T(1,128)S(1)} %stack_reshape_squeeze.7), channel_id=1, source_target_pairs={{8,0},{16,8},{24,16},{32,24},{40,32},{48,40},{56,48},{64,56},{72,6... | collective-permute-start | bytes 52232 | tf_op jit(solution)/shard_map/ppermute | solution.py:23
  34.3 81.5 %collective-permute-start = (f32[1,17,256]{2,0,1:T(1,128)S(1)}, f32[1,17,256]{2,0,1:T(1,128)}, u32[]{:S(2)}, u32[]{:S(2)}) collective-permute-start(f32[1,17,256]{2,0,1:T(1,128)S(1)} %copy.46), channel_id=1, source_target_pairs={{0,8},{8,16},{16,24},{24,32},{32,40},{40,48},{48,56},{56,64},{64,7... | collective-permute-start | bytes 52232 | tf_op jit(solution)/shard_map/ppermute | solution.py:20
  52.5 76.8 %collective-permute-start.2 = (f32[1,6,17,256]{3,0,2,1:T(1,128)}, f32[1,6,17,256]{3,0,2,1:T(1,128)}, u32[]{:S(2)}, u32[]{:S(2)}) collective-permute-start(f32[1,6,17,256]{3,0,2,1:T(1,128)} %copy.47), channel_id=1, source_target_pairs={{0,1},{1,2},{2,3},{3,4},{4,5},{5,6},{6,7},{8,9},{9,10},{10,11},{11... | collective-permute-start | bytes 313352 | tf_op jit(solution)/shard_map/ppermute | solution.py:20
  58.6 21.2 %slice-start = ((s8[13369344]{0:T(1024)(128)(4,1)}), s8[4194304]{0:T(1024)(128)(4,1)S(1)}, s32[]{:S(2)}) async-start(s8[13369344]{0:T(1024)(128)(4,1)} %bitcast.138), calls=%async_computation.1 | async-start | bytes 8388608
  59.3 20.5 %slice-start.1 = ((s8[13369344]{0:T(1024)(128)(4,1)}), s8[4194304]{0:T(1024)(128)(4,1)S(1)}, s32[]{:S(2)}) async-start(s8[13369344]{0:T(1024)(128)(4,1)} %bitcast.138), calls=%async_computation.2 | async-start | bytes 8388608
  59.3 20.5 %slice-start.2 = ((s8[13369344]{0:T(1024)(128)(4,1)}), s8[4194304]{0:T(1024)(128)(4,1)S(1)}, s32[]{:S(2)}) async-start(s8[13369344]{0:T(1024)(128)(4,1)} %bitcast.138), calls=%async_computation.3 | async-start | bytes 8388608
  59.3 20.5 %slice-start.3 = ((s8[13369344]{0:T(1024)(128)(4,1)}), s8[786432]{0:T(1024)(128)(4,1)S(1)}, s32[]{:S(2)}) async-start(s8[13369344]{0:T(1024)(128)(4,1)} %bitcast.138), calls=%async_computation.4 | async-start | bytes 1572864
  59.3 64.3 %collective-permute-start.3 = (f32[1,6,17,256]{3,0,2,1:T(1,128)}, f32[1,6,17,256]{3,0,2,1:T(1,128)}, u32[]{:S(2)}, u32[]{:S(2)}) collective-permute-start(f32[1,6,17,256]{3,0,2,1:T(1,128)} %copy.48), channel_id=1, source_target_pairs={{1,0},{2,1},{3,2},{4,3},{5,4},{6,5},{7,6},{9,8},{10,9},{11,10},{12... | collective-permute-start | bytes 313352 | tf_op jit(solution)/shard_map/ppermute | solution.py:23
  100.1 5.1 copy-start.3
  101.5 5.2 copy-start.4
  102.8 5.4 copy-start.8
  102.8 5.5 copy-start.16
  116.7 5.6 copy-start.6
  177.1 10.5 %copy-start.13 = (f32[6]{0:T(128)S(1)}, f32[6]{0:T(128)}, u32[]{:S(2)}) copy-start(f32[6]{0:T(128)} %copy-done.12) | copy-start | bytes 76
  272.3 5.3 copy-start.1
  272.3 5.3 copy-start.2
  287.3 9.7 %copy-start.10 = (s32[2048]{0:T(1024)S(1)}, s32[2048]{0:T(1024)}, u32[]{:S(2)}) copy-start(s32[2048]{0:T(1024)} %get-tuple-element.33) | copy-start | bytes 24580
  297.0 21.6 %copy-start.7 = (f32[2048,6]{1,0:T(8,128)S(1)}, f32[2048,6]{1,0:T(8,128)}, u32[]{:S(2)}) copy-start(f32[2048,6]{1,0:T(8,128)} %copy.53) | copy-start | bytes 147460
  297.0 21.6 %copy-start.15 = (pred[2048]{0:T(1024)(128)(4,1)S(1)}, pred[2048]{0:T(1024)(128)(4,1)}, u32[]{:S(2)}) copy-start(pred[2048]{0:T(1024)(128)(4,1)} %compare_and_fusion) | copy-start | bytes 6148
  318.6 266.7 %copy-start.14 = (f32[16,16]{1,0:T(8,128)S(1)}, f32[16,16]{1,0:T(8,128)}, u32[]{:S(2)}) copy-start(f32[16,16]{1,0:T(8,128)} %param.13) | copy-start | bytes 3076
  (2 other events, 5.1 us)
Sparse Core Ops, SparseCore 0:
  333.1 247.8 all-reduce.6
where the time goes:
time: 612 us; the launch traced here: 604 us
  waiting for transfers between devices  248 us (41%)
  local copies, waits for them, and re-layouts  139 us (23%)
  other arithmetic  81.1 us (13%)
  blocking collectives  80 us (13%)
  matrix products  25.8 us (4%)
  between operations  16.2 us (3%)
  starting transfers between devices  14.1 us (2%)
    psum x1, waiting for transfers between devices, body(): sketch_whole = lax.psum(partial_value, ('px', 'py'))  248 us
    psum x1, blocking collectives, body(): proj_coef = lax.psum(local_gram, ('px', 'py')) / total_cells  80 us
    sub x1, other arithmetic, apply_operator(): summed = diag_sum * centre_vals - weighted  37.8 us
    slice x2, local copies, waits for them, and re-layouts, shift_pair(): lax.slice_in_dim(cube_vals, 1, PS, axis=axis_pos)  26.7 us
    gather x1, local copies, waits for them, and re-layouts, body(): picked = jnp.take(spread, sample_rows % CELLS, axis=2)  21.6 us
    slice x4, local copies, waits for them, and re-layouts, shift_pair(): lax.slice_in_dim(cube_vals, 0, PS - 1, axis=axis_pos)  13.8 us
    unnamed x3, other arithmetic  13.3 us
  transfers between devices with their start and end apart: 5, of which 1 were waited for; matrix products, arithmetic and copies ran while one was open for 15% of the time, Pallas kernels for 0%

commit v1 on v0

--- a/solution.py
+++ b/solution.py
@@ -161,7 +161,7 @@
     partial_value = jnp.einsum("sk,sjk->jk", weights, picked, precision=highest) * (
         1.0 / math.sqrt(total_cells)
     )
-    sketch_whole = lax.psum(partial_value, ("px", "py"))
+    sketch_whole = lax.psum(lax.psum(partial_value, "px"), "py")
     sketch_mine = lax.dynamic_slice_in_dim(sketch_whole, share_start, share_width, 1)
     normal_gram, normal_cross = normal_parts(
         sketch_whole, proj_coef, previous_coef, residual_factor

time: 612 us -> 572 us (0.935)
  waiting for transfers between devices: 248 us -> 207 us
    psum x1 -> x2, waiting for transfers between devices: 248 us -> 207 us  [body(): sketch_whole = lax.psum(lax.psum(partial_value, 'px'), 'py')]
  transfers between devices with their start and end apart: 5 -> 6, of which waited for: 1 -> 2; matrix products, arithmetic and copies ran while one was open for 15% -> 16% of each run, Pallas kernels for 0% -> 0%
where the time goes in v1:
time: 572 us; the launch traced here: 563 us
  waiting for transfers between devices  207 us (36%)
  local copies, waits for them, and re-layouts  139 us (24%)
  other arithmetic  81.1 us (14%)
  blocking collectives  80 us (14%)
  matrix products  25.8 us (5%)
  between operations  16.2 us (3%)
  starting transfers between devices  14.1 us (2%)
    psum x2, waiting for transfers between devices, body(): sketch_whole = lax.psum(lax.psum(partial_value, 'px'), 'py')  207 us
    psum x1, blocking collectives, body(): proj_coef = lax.psum(local_gram, ('px', 'py')) / total_cells  80 us
    sub x1, other arithmetic, apply_operator(): summed = diag_sum * centre_vals - weighted  37.8 us
    slice x2, local copies, waits for them, and re-layouts, shift_pair(): lax.slice_in_dim(cube_vals, 1, PS, axis=axis_pos)  26.7 us
    gather x1, local copies, waits for them, and re-layouts, body(): picked = jnp.take(spread, sample_rows % CELLS, axis=2)  21.6 us
    slice x4, local copies, waits for them, and re-layouts, shift_pair(): lax.slice_in_dim(cube_vals, 0, PS - 1, axis=axis_pos)  13.8 us
    unnamed x3, other arithmetic  13.3 us
  transfers between devices with their start and end apart: 6, of which 2 were waited for; matrix products, arithmetic and copies ran while one was open for 16% of the time, Pallas kernels for 0%

profile of v1, /device:TPU:1, one launch (start us, length us, event | category | flops | bytes accessed | tf_op | source)
XLA Modules:
  0.0 562.5 jit_solution(17391844290049469332)
XLA Ops:
  14.0 8.6 %reshape.92 = f32[6,17,16,16,16]{4,3,2,0,1:T(8,128)} reshape(f32[6,17,4096]{2,0,1:T(8,128)} %copy.21) | data formatting | bytes 3342336 | tf_op jit(solution)/shard_map/reshape | solution.py:69
  26.3 3.2 constant_dynamic-slice_fusion.1
  29.5 3.9 copy.22
  34.3 5.2 collective-permute-start
  39.5 10.8 %slice_reduce_fusion = (f32[6,17,16,16]{3,2,0,1:T(8,128)}, f32[6,17,16,16]{3,2,0,1:T(8,128)}) fusion(f32[6,17,16,16,16]{4,3,2,0,1:T(8,128)} %reshape.92), kind=kLoop, calls=%fused_computation.34 | loop fusion | bytes 417792 | tf_op jit(solution)/shard_map/slice | solution.py:74
  52.5 4.6 collective-permute-start.2
  62.4 17.5 %fusion.102 = (f32[6,16,15,16,16]{4,3,2,0,1:T(8,128)}, f32[6,16,15,16,16]{4,3,2,0,1:T(8,128)}) fusion(f32[6,17,16,16,16]{4,3,2,0,1:T(8,128)} %reshape.92), kind=kLoop, calls=%fused_computation.173 | loop fusion | bytes 5898240 | tf_op jit(solution)/shard_map/slice | solution.py:59
  81.1 9.2 %fusion.101 = (f32[6,16,16,15,16]{4,3,2,0,1:T(8,128)}, f32[6,16,16,15,16]{4,3,2,0,1:T(8,128)}) fusion(f32[6,17,16,16,16]{4,3,2,0,1:T(8,128)S(1)} %bitcast.139), kind=kLoop, calls=%fused_computation.172 | loop fusion | bytes 5898240 | tf_op jit(solution)/shard_map/slice | solution.py:59
  90.3 9.8 %fusion.100 = (f32[6,16,16,16,15]{4,3,2,0,1:T(8,128)}, f32[6,16,16,16,15]{4,3,2,0,1:T(8,128)}) fusion(f32[6,17,16,16,16]{4,3,2,0,1:T(8,128)S(1)} %bitcast.139), kind=kLoop, calls=%fused_computation.171 | loop fusion | bytes 5898240 | tf_op jit(solution)/shard_map/slice | solution.py:54
  109.1 4.0 bitcast_multiply_fusion.1
  118.9 3.5 fusion.30
  134.3 5.0 add_bitcast_fusion
  139.3 37.8 %fusion = f32[6,16,16,16,16]{4,3,2,0,1:T(8,128)} fusion(f32[6,17,16,16,16]{4,3,2,0,1:T(8,128)} %reshape.92, f32[6,16,15,16,16]{4,3,2,0,1:T(8,128)} %get-tuple-element.29, f32[6,16,1,16,16]{4,3,2,0,1:T(8,128)} %get-tuple-element.41, f32[6,16,1,16,16]{4,3,2,0,1:T(8,128)} %get-tuple-element.40, f32[6,16,15,16,16]{4,3,2,0,1:T(8,128)} %get-tuple-element.28, ...), kind=kLoop, calls=%fused_computation.2 | loop fusion | flops 6684672 | bytes 13074432 | tf_op jit(solution)/shard_map/sub | solution.py:103
  177.1 10.5 %reshape.114 = f32[6,16,4096]{2,0,1:T(8,128)} reshape(f32[6,16,16,16,16]{4,3,2,0,1:T(8,128)} %fusion) | data formatting | bytes 3145728 | tf_op jit(solution)/shard_map/reshape | solution.py:104
  187.6 4.7 fusion.14
  192.3 80.0 %psum.21 = f32[32,16]{0,1:T(8,128)S(1)} all-reduce(f32[32,16]{0,1:T(8,128)S(1)} %fusion.14), channel_id=1, replica_groups=mesh['px'=32,'py'=8] {'px','py'}, use_global_device_ids=true, to_apply=%region_0.0 | all-reduce | flops 512 | bytes 4096 | tf_op jit(solution)/shard_map/psum | solution.py:155
  272.4 4.1 fusion.6
  277.6 4.0 fusion.7
  281.7 5.7 %convolution_bitcast_fusion.1 = f32[6,48,32,128]{3,2,1,0:T(8,128)} fusion(f32[6,48,32,128]{3,2,1,0:T(8,128)S(1)} %fusion.7), kind=kOutput, calls=%fused_computation.25 | convolution fusion | flops 453000192 | bytes 9437184 | tf_op jit(solution)/shard_map/ca,sjad->sjcd/dot_general | solution.py:46
  287.3 9.7 %copy.50 = f32[6,48,32,128]{1,0,3,2:T(8,128)} copy(f32[6,48,32,128]{3,2,1,0:T(8,128)} %convolution_bitcast_fusion.1) | data formatting | bytes 9437184 | tf_op jit(solution)/shard_map/reshape | solution.py:47
  297.0 21.6 %gather_fusion = f32[2048,6,48]{2,1,0:T(8,128)} fusion(f32[6,48,4096]{1,0,2:T(8,128)} %bitcast.140, s32[2048]{0:T(1024)S(1)} %copy-done.10), kind=kCustom, calls=%fused_computation | custom fusion | bytes 4726784 | tf_op jit(solution)/shard_map/jit(_take)/gather | solution.py:158
  318.7 13.2 %multiply_reduce_fusion = f32[2048,48]{1,0:T(8,128)S(1)} fusion(f32[2048,6,48]{2,1,0:T(8,128)} %gather_fusion, f32[2048,6]{1,0:T(8,128)S(1)} %copy-done.7, pred[2048]{0:T(1024)(128)(4,1)S(1)} %copy-done.15), kind=kLoop, calls=%fused_computation.12 | loop fusion | flops 1671168 | bytes 2803712
  333.1 138.6 %all-reduce.8.cloned.1.call-done = f32[48,2048]{1,0:T(8,128)} async-done(((f32[48,2048]{1,0:T(8,128)}), f32[48,2048]{1,0:T(8,128)}) %all-reduce.8.cloned.1.call-update) | async-done | bytes 393232 | tf_op jit(solution)/shard_map/psum | solution.py:164
  471.7 68.0 %all-reduce.10.cloned.1.call-done = f32[48,2048]{1,0:T(8,128)} async-done(((f32[48,2048]{1,0:T(8,128)}), f32[48,2048]{1,0:T(8,128)}) %all-reduce.10.cloned.1.call-update) | async-done | bytes 393232 | tf_op jit(solution)/shard_map/psum | solution.py:164
  (118 shorter events, 63.2 us)
Async XLA Ops:
  7.2 535.2 %copy-start = (f32[32,16]{0,1:T(8,128)S(1)}, f32[32,16]{0,1:T(8,128)}, u32[]{:S(2)}) copy-start(f32[32,16]{0,1:T(8,128)} %param.14) | copy-start | bytes 6148
  7.2 464.5 %all-reduce.8.cloned.1.call-start = ((), (), s32[]{:S(2)}) async-start(), calls=%async_computation | async-start | bytes 786432 | tf_op jit(solution)/shard_map/psum | solution.py:164
  9.1 104.6 %copy-start.12 = (f32[6]{0:T(128)}, f32[6]{0:T(128)S(1)}, u32[]{:S(2)}) copy-start(f32[6]{0:T(128)S(1)} %compare_convert_fusion) | copy-start | bytes 76
  23.7 92.0 %collective-permute-start.1 = (f32[1,17,256]{2,0,1:T(1,128)S(1)}, f32[1,17,256]{2,0,1:T(1,128)S(1)}, u32[]{:S(2)}, u32[]{:S(2)}) collective-permute-start(f32[1,17,256]{2,0,1:T(1,128)S(1)} %stack_reshape_squeeze.7), channel_id=1, source_target_pairs={{8,0},{16,8},{24,16},{32,24},{40,32},{48,40},{56,48},{64,56},{72,6... | collective-permute-start | bytes 52232 | tf_op jit(solution)/shard_map/ppermute | solution.py:23
  34.3 81.5 %collective-permute-start = (f32[1,17,256]{2,0,1:T(1,128)S(1)}, f32[1,17,256]{2,0,1:T(1,128)}, u32[]{:S(2)}, u32[]{:S(2)}) collective-permute-start(f32[1,17,256]{2,0,1:T(1,128)S(1)} %copy.46), channel_id=1, source_target_pairs={{0,8},{8,16},{16,24},{24,32},{32,40},{40,48},{48,56},{56,64},{64,7... | collective-permute-start | bytes 52232 | tf_op jit(solution)/shard_map/ppermute | solution.py:20
  52.5 76.8 %collective-permute-start.2 = (f32[1,6,17,256]{3,0,2,1:T(1,128)}, f32[1,6,17,256]{3,0,2,1:T(1,128)}, u32[]{:S(2)}, u32[]{:S(2)}) collective-permute-start(f32[1,6,17,256]{3,0,2,1:T(1,128)} %copy.47), channel_id=1, source_target_pairs={{0,1},{1,2},{2,3},{3,4},{4,5},{5,6},{6,7},{8,9},{9,10},{10,11},{11... | collective-permute-start | bytes 313352 | tf_op jit(solution)/shard_map/ppermute | solution.py:20
  58.6 21.2 %slice-start = ((s8[13369344]{0:T(1024)(128)(4,1)}), s8[4194304]{0:T(1024)(128)(4,1)S(1)}, s32[]{:S(2)}) async-start(s8[13369344]{0:T(1024)(128)(4,1)} %bitcast.138), calls=%async_computation.2 | async-start | bytes 8388608
  59.3 20.5 %slice-start.1 = ((s8[13369344]{0:T(1024)(128)(4,1)}), s8[4194304]{0:T(1024)(128)(4,1)S(1)}, s32[]{:S(2)}) async-start(s8[13369344]{0:T(1024)(128)(4,1)} %bitcast.138), calls=%async_computation.3 | async-start | bytes 8388608
  59.3 20.5 %slice-start.2 = ((s8[13369344]{0:T(1024)(128)(4,1)}), s8[4194304]{0:T(1024)(128)(4,1)S(1)}, s32[]{:S(2)}) async-start(s8[13369344]{0:T(1024)(128)(4,1)} %bitcast.138), calls=%async_computation.4 | async-start | bytes 8388608
  59.3 20.5 %slice-start.3 = ((s8[13369344]{0:T(1024)(128)(4,1)}), s8[786432]{0:T(1024)(128)(4,1)S(1)}, s32[]{:S(2)}) async-start(s8[13369344]{0:T(1024)(128)(4,1)} %bitcast.138), calls=%async_computation.5 | async-start | bytes 1572864
  59.3 64.3 %collective-permute-start.3 = (f32[1,6,17,256]{3,0,2,1:T(1,128)}, f32[1,6,17,256]{3,0,2,1:T(1,128)}, u32[]{:S(2)}, u32[]{:S(2)}) collective-permute-start(f32[1,6,17,256]{3,0,2,1:T(1,128)} %copy.48), channel_id=1, source_target_pairs={{1,0},{2,1},{3,2},{4,3},{5,4},{6,5},{7,6},{9,8},{10,9},{11,10},{12... | collective-permute-start | bytes 313352 | tf_op jit(solution)/shard_map/ppermute | solution.py:23
  100.1 5.1 copy-start.3
  101.5 5.2 copy-start.4
  102.8 5.4 copy-start.8
  102.8 5.5 copy-start.16
  116.7 5.6 %copy-start.6 = (f32[5,17,16,16]{3,2,0,1:T(8,128)S(1)}, f32[5,17,16,16]{3,2,0,1:T(8,128)}, u32[]{:S(2)}) copy-start(f32[5,17,16,16]{3,2,0,1:T(8,128)} %get-tuple-element.31) | copy-start | bytes 261124
  177.1 10.5 %copy-start.13 = (f32[6]{0:T(128)S(1)}, f32[6]{0:T(128)}, u32[]{:S(2)}) copy-start(f32[6]{0:T(128)} %copy-done.12) | copy-start | bytes 76
  272.4 5.3 copy-start.1
  272.4 5.3 copy-start.2
  287.3 9.7 %copy-start.10 = (s32[2048]{0:T(1024)S(1)}, s32[2048]{0:T(1024)}, u32[]{:S(2)}) copy-start(s32[2048]{0:T(1024)} %get-tuple-element.33) | copy-start | bytes 24580
  297.0 21.6 %copy-start.7 = (f32[2048,6]{1,0:T(8,128)S(1)}, f32[2048,6]{1,0:T(8,128)}, u32[]{:S(2)}) copy-start(f32[2048,6]{1,0:T(8,128)} %copy.53) | copy-start | bytes 147460
  297.0 21.6 %copy-start.15 = (pred[2048]{0:T(1024)(128)(4,1)S(1)}, pred[2048]{0:T(1024)(128)(4,1)}, u32[]{:S(2)}) copy-start(pred[2048]{0:T(1024)(128)(4,1)} %compare_and_fusion) | copy-start | bytes 6148
  318.6 225.4 %copy-start.14 = (f32[16,16]{1,0:T(8,128)S(1)}, f32[16,16]{1,0:T(8,128)}, u32[]{:S(2)}) copy-start(f32[16,16]{1,0:T(8,128)} %param.13) | copy-start | bytes 3076
  333.0 206.7 %all-reduce.10.cloned.1.call-start = ((), (), s32[]{:S(2)}) async-start(), calls=%async_computation.1 | async-start | bytes 786432 | tf_op jit(solution)/shard_map/psum | solution.py:164
  (3 other events, 9.3 us)
Sparse Core Ops, SparseCore 0:
  333.1 138.5 all-reduce.7
  474.0 65.6 all-reduce.9
